TPU v7x, 32 devices: a whole 2x2x4 slice. The times are simulated.
32 devices in a mesh: pipe: 4 (over z), expert: 8 (over y, x, core).
Axes of the slice: x: 2, y: 2, z: 4, core: 2. Of those that a mesh axis runs over, the one named last changes fastest.
Arguments:
- fwd_state: bfloat16 [4, 192, 3584], P('pipe', 'expert'), may hold values from -6 to 6
- bwd_state: bfloat16 [4, 192, 3584], P('pipe', 'expert'), may hold values from -6 to 6
- saved_input: bfloat16 [4, 2, 192, 3584], P('pipe', None, 'expert'), may hold values from -6 to 6
- fwd_route: int32 [4, 2, 192, 1], P('pipe', None, 'expert'), may hold values from 0 to 3; in each aligned block of 24 rows (0 to 23, 24 to 47, ..., all dimensions but the last counted through in order) at most 7 rows name the same one
- bwd_route: int32 [4, 2, 192, 1], P('pipe', None, 'expert'), may hold values from 0 to 3; in each aligned block of 24 rows (0 to 23, 24 to 47, ..., all dimensions but the last counted through in order) at most 7 rows name the same one
- fwd_gate: float32 [4, 2, 192], P('pipe', None, 'expert'), may hold values from 0.3 to 1
- bwd_gate: float32 [4, 2, 192], P('pipe', None, 'expert'), may hold values from 0.3 to 1
- w_gate: bfloat16 [4, 3584, 1024], P('pipe', None, 'expert'), may hold values from -0.09375 to 0.09375
- w_up: bfloat16 [4, 3584, 1024], P('pipe', None, 'expert'), may hold values from -0.09375 to 0.09375
- w_down: bfloat16 [4, 1024, 3584], P('pipe', 'expert'), may hold values from -0.375 to 0.375
- norm_gain: float32 [4, 3584], P('pipe'), may hold values from 0.5 to 1.5
Outputs:
- fwd_out: bfloat16 [4, 192, 3584], P('pipe', 'expert')
- bwd_out: bfloat16 [4, 192, 3584], P('pipe', 'expert')
Inputs may be any that keep to these rules, and one draw needn't show every extreme that they name: `fwd_route`: in the rows of one device at one rank and step, no expert is named more than 7 times, and one is named exactly 7 times. `bwd_route`: as for fwd_route.
All inputs are finite; a program needn't handle non-finite values.
Results may differ from a plain program's by a relative error of at most 0.0068.
Values may be sent and summed in bfloat16 or wider, within the bound.
No kernel may reach another device: no remote copies, remote signals or barrier semaphores. Data moves between devices by JAX's collectives and lax.ppermute only.
A program may use at most 64 MiB of HBM per device.

v0:
```python
import jax
import jax.numpy as jnp
from jax import lax
from jax.sharding import PartitionSpec as P

EXPERTS = 4
CAP = 7
EPS = 1e-06


def passed_along(array, axis, by):
    size = lax.axis_size(axis)
    pairs = [(i, i + by) for i in range(size) if 0 <= i + by < size]
    return lax.ppermute(array, axis, pairs)


def norm_rows(rows, gain):
    raw = rows.astype(jnp.float32)
    scale = lax.rsqrt(jnp.mean(raw * raw, axis=-1, keepdims=True) + EPS)
    return (raw, scale, (raw * scale * gain).astype(jnp.bfloat16))


def slot_index(route):
    hits = (route[:, None] == jnp.arange(EXPERTS, dtype=jnp.int32)[None, :]).astype(jnp.int32)
    before = jnp.cumsum(hits, axis=0) - hits
    return route * CAP + jnp.sum(before * hits, axis=1)


def slot_table(index):
    columns = jnp.arange(EXPERTS * CAP, dtype=jnp.int32)
    return (columns[:, None] == index[None, :]).astype(jnp.bfloat16)


def fill_slots(table, rows, shards):
    picked = jnp.dot(table, rows, preferred_element_type=jnp.float32).astype(jnp.bfloat16)
    return jnp.repeat(picked.reshape(EXPERTS, CAP, rows.shape[1]), shards, axis=0)


def collect_rows(returned, index, shards):
    width = returned.shape[2]
    summed = (
        returned.reshape(EXPERTS, shards, returned.shape[1], width).astype(jnp.float32).sum(axis=1)
    )
    return jnp.take(summed.reshape(EXPERTS * CAP, width), index, axis=0)


def local(
    fwd_state,
    bwd_state,
    saved_input,
    fwd_route,
    bwd_route,
    fwd_gate,
    bwd_gate,
    w_gate,
    w_up,
    w_down,
    norm_gain,
):
    shards = lax.axis_size("expert") // EXPERTS
    gain = norm_gain[0]
    gate_cols = w_gate[0]
    up_cols = w_up[0]
    down_rows = w_down[0]
    steps_total = fwd_route.shape[1]
    forward = fwd_state[0]
    backward = bwd_state[0]
    new_forward = forward
    new_backward = backward
    for moment in range(steps_total):
        fwd_index = slot_index(fwd_route[0, moment, :, 0])
        fwd_raw, fwd_scale, fwd_norm = norm_rows(forward, gain)
        fwd_slots = fill_slots(slot_table(fwd_index), fwd_norm, shards)
        bwd_index = slot_index(bwd_route[0, moment, :, 0])
        bwd_table = slot_table(bwd_index)
        bwd_raw, bwd_scale, bwd_norm = norm_rows(saved_input[0, moment], gain)
        scaled = (bwd_gate[0, moment][:, None] * backward.astype(jnp.float32)).astype(jnp.bfloat16)
        bwd_inputs = fill_slots(bwd_table, bwd_norm, shards)
        bwd_grads = fill_slots(bwd_table, scaled, shards)
        expert_received = lax.all_to_all(
            fwd_slots, "expert", split_axis=0, concat_axis=0, tiled=True
        )
        expert_gated = jnp.einsum(
            "scd,dh->sch", expert_received, gate_cols, preferred_element_type=jnp.float32
        )
        expert_upped = jnp.einsum(
            "scd,dh->sch", expert_received, up_cols, preferred_element_type=jnp.float32
        )
        hidden = (expert_gated * jax.nn.sigmoid(expert_gated) * expert_upped).astype(jnp.bfloat16)
        fwd_partial = jnp.einsum(
            "sch,hd->scd", hidden, down_rows, preferred_element_type=jnp.float32
        ).astype(jnp.bfloat16)
        fwd_back = lax.all_to_all(fwd_partial, "expert", split_axis=0, concat_axis=0, tiled=True)
        inputs_part = lax.all_to_all(bwd_inputs, "expert", split_axis=0, concat_axis=0, tiled=True)
        grads_part = lax.all_to_all(bwd_grads, "expert", split_axis=0, concat_axis=0, tiled=True)
        gated = jnp.einsum(
            "scd,dh->sch", inputs_part, gate_cols, preferred_element_type=jnp.float32
        )
        upped = jnp.einsum("scd,dh->sch", inputs_part, up_cols, preferred_element_type=jnp.float32)
        dhidden = jnp.einsum(
            "scd,hd->sch", grads_part, down_rows, preferred_element_type=jnp.float32
        )
        sigma = jax.nn.sigmoid(gated)
        dgate = (dhidden * upped * sigma * (1.0 + gated * (1.0 - sigma))).astype(jnp.bfloat16)
        dup = (dhidden * gated * sigma).astype(jnp.bfloat16)
        result = jnp.einsum("sch,dh->scd", dgate, gate_cols, preferred_element_type=jnp.float32)
        result = result + jnp.einsum(
            "sch,dh->scd", dup, up_cols, preferred_element_type=jnp.float32
        )
        bwd_partial = result.astype(jnp.bfloat16)
        bwd_back = lax.all_to_all(bwd_partial, "expert", split_axis=0, concat_axis=0, tiled=True)
        moe_rows = collect_rows(fwd_back, fwd_index, shards)
        new_forward = (fwd_raw + fwd_gate[0, moment][:, None] * moe_rows).astype(jnp.bfloat16)
        dnorm = collect_rows(bwd_back, bwd_index, shards)
        weighted = gain * dnorm
        cubed = bwd_scale * bwd_scale * bwd_scale
        dinput = bwd_scale * weighted - bwd_raw * cubed * jnp.mean(
            bwd_raw * weighted, axis=-1, keepdims=True
        )
        new_backward = (backward.astype(jnp.float32) + dinput).astype(jnp.bfloat16)
        if moment + 1 < steps_total:
            forward = passed_along(new_forward, "pipe", 1)
            backward = passed_along(new_backward, "pipe", -1)
    return (new_forward[None], new_backward[None])


def solution(mesh):
    placed = (
        P("pipe", "expert", None),
        P("pipe", "expert", None),
        P("pipe", None, "expert", None),
        P("pipe", None, "expert", None),
        P("pipe", None, "expert", None),
        P("pipe", None, "expert"),
        P("pipe", None, "expert"),
        P("pipe", None, "expert"),
        P("pipe", None, "expert"),
        P("pipe", "expert", None),
        P("pipe", None),
    )
    return jax.shard_map(
        local,
        mesh=mesh,
        in_specs=placed,
        out_specs=(P("pipe", "expert", None), P("pipe", "expert", None)),
        check_vma=False,
    )
```

profile of v0, /device:TPU:0, one launch (start us, length us, event | category | flops | bytes accessed | tf_op | source)
XLA Modules:
  0.0 158.4 jit_solution(18121276886140860241)
XLA Ops:
  6.8 5.3 %all-to-all-start.5 = ((bf16[8,7,3584]{2,1,0:T(8,128)(2,1)}), bf16[8,7,3584]{2,1,0:T(8,128)(2,1)S(1)}, u32[]{:S(2)}, u32[]{:S(2)}) async-start(bf16[8,7,3584]{2,1,0:T(8,128)(2,1)} %bitcast.24), calls=%async_computation.5 | async-start | bytes 917504 | tf_op jit(solution)/shard_map/all_to_all | solution.py:94
  19.1 2.1 %all-to-all-done.5 = bf16[8,7,3584]{2,1,0:T(8,128)(2,1)S(1)} async-done(((bf16[8,7,3584]{2,1,0:T(8,128)(2,1)}), bf16[8,7,3584]{2,1,0:T(8,128)(2,1)S(1)}, u32[]{:S(2)}, u32[]{:S(2)}) %all-to-all-start.5) | async-done | bytes 401440 | tf_op jit(solution)/shard_map/all_to_all | solution.py:94
  22.0 3.5 %all-to-all-start.4 = ((bf16[8,7,3584]{2,1,0:T(8,128)(2,1)}), bf16[8,7,3584]{2,1,0:T(8,128)(2,1)S(1)}, u32[]{:S(2)}, u32[]{:S(2)}) async-start(bf16[8,7,3584]{2,1,0:T(8,128)(2,1)} %bitcast.22), calls=%async_computation.4 | async-start | bytes 917504 | tf_op jit(solution)/shard_map/all_to_all | solution.py:95
  26.1 8.3 %all-to-all-done.4 = bf16[8,7,3584]{2,1,0:T(8,128)(2,1)S(1)} async-done(((bf16[8,7,3584]{2,1,0:T(8,128)(2,1)}), bf16[8,7,3584]{2,1,0:T(8,128)(2,1)S(1)}, u32[]{:S(2)}, u32[]{:S(2)}) %all-to-all-start.4) | async-done | bytes 401440 | tf_op jit(solution)/shard_map/all_to_all | solution.py:95
  35.3 3.5 %all-to-all-start = ((bf16[8,7,3584]{2,1,0:T(8,128)(2,1)}), bf16[8,7,3584]{2,1,0:T(8,128)(2,1)S(1)}, u32[]{:S(2)}, u32[]{:S(2)}) async-start(bf16[8,7,3584]{2,1,0:T(8,128)(2,1)} %bitcast.131), calls=%async_computation | async-start | bytes 917504 | tf_op jit(solution)/shard_map/all_to_all | solution.py:80
  38.8 1.5 fusion.4
  42.1 5.7 %all-to-all-done = bf16[8,7,3584]{2,1,0:T(8,128)(2,1)S(1)} async-done(((bf16[8,7,3584]{2,1,0:T(8,128)(2,1)}), bf16[8,7,3584]{2,1,0:T(8,128)(2,1)S(1)}, u32[]{:S(2)}, u32[]{:S(2)}) %all-to-all-start) | async-done | bytes 401440 | tf_op jit(solution)/shard_map/all_to_all | solution.py:80
  47.8 4.1 %all-to-all-start.6 = ((bf16[8,7,3584]{2,1,0:T(8,128)(2,1)}), bf16[8,7,3584]{2,1,0:T(8,128)(2,1)}, u32[]{:S(2)}, u32[]{:S(2)}) async-start(bf16[8,7,3584]{2,1,0:T(8,128)(2,1)} %copy.38), calls=%async_computation.6 | async-start | bytes 917504 | tf_op jit(solution)/shard_map/all_to_all | solution.py:111
  53.7 7.2 %all-to-all-done.6 = bf16[8,7,3584]{2,1,0:T(8,128)(2,1)} async-done(((bf16[8,7,3584]{2,1,0:T(8,128)(2,1)}), bf16[8,7,3584]{2,1,0:T(8,128)(2,1)}, u32[]{:S(2)}, u32[]{:S(2)}) %all-to-all-start.6) | async-done | bytes 401440 | tf_op jit(solution)/shard_map/all_to_all | solution.py:111
  60.9 4.1 %all-to-all-start.1 = ((bf16[8,7,3584]{2,1,0:T(8,128)(2,1)}), bf16[8,7,3584]{2,1,0:T(8,128)(2,1)}, u32[]{:S(2)}, u32[]{:S(2)}) async-start(bf16[8,7,3584]{2,1,0:T(8,128)(2,1)} %copy.27), calls=%async_computation.1 | async-start | bytes 917504 | tf_op jit(solution)/shard_map/all_to_all | solution.py:93
  65.0 1.9 %convert_reduce_fusion.1 = f32[4,7,3584]{2,1,0:T(8,128)} fusion(bf16[8,7,3584]{2,1,0:T(8,128)(2,1)} %all-to-all-done.6), kind=kLoop, calls=%fused_computation.17 | loop fusion | flops 301056 | bytes 802816 | tf_op jit(solution)/shard_map/reduce_sum | solution.py:42
  68.1 1.7 %gather_fusion.2 = f32[24,3584]{1,0:T(8,128)} fusion(f32[28,3584]{1,0:T(8,128)S(1)} %reshape.179, s32[1024]{0:T(1024)} %pad_clamp_fusion.1), kind=kCustom, calls=%fused_computation.2.clone | custom fusion | bytes 688224 | tf_op jit(solution)/shard_map/jit(_take)/gather | solution.py:44
  76.8 4.1 %all-to-all-start.8 = ((bf16[8,7,3584]{2,1,0:T(8,128)(2,1)}), bf16[8,7,3584]{2,1,0:T(8,128)(2,1)}, u32[]{:S(2)}, u32[]{:S(2)}) async-start(bf16[8,7,3584]{2,1,0:T(8,128)(2,1)} %bitcast.31), calls=%async_computation.8 | async-start | bytes 917504 | tf_op jit(solution)/shard_map/all_to_all | solution.py:94
  80.9 1.9 %convert_reduce_fusion.3 = f32[4,7,3584]{2,1,0:T(8,128)} fusion(bf16[8,7,3584]{2,1,0:T(8,128)(2,1)} %all-to-all-done.1), kind=kLoop, calls=%fused_computation.19 | loop fusion | flops 301056 | bytes 802816 | tf_op jit(solution)/shard_map/reduce_sum | solution.py:42
  83.9 1.5 gather_fusion
  86.1 1.8 %fusion.41 = bf16[24,3584]{1,0:T(8,128)(2,1)} fusion(f32[24,3584]{1,0:T(8,128)} %gather_fusion, bf16[1,24,3584]{2,1,0:T(8,128)(2,1)} %param.13, f32[24]{0:T(128)S(1)} %copy-done.34, pred[24]{0:T(512)(128)(4,1)S(1)} %copy-done.36), kind=kLoop, calls=%fused_computation.77 | loop fusion | flops 430080 | bytes 688248 | tf_op jit(solution)/shard_map/convert_element_type | solution.py:113
  88.0 4.7 %collective-permute-start = (bf16[24,3584]{1,0:T(8,128)(2,1)}, bf16[24,3584]{1,0:T(8,128)(2,1)S(1)}, u32[]{:S(2)}, u32[]{:S(2)}) collective-permute-start(bf16[24,3584]{1,0:T(8,128)(2,1)} %fusion.41), channel_id=1, source_target_pairs={{0,8},{8,16},{16,24},{1,9},{9,17},{17,25},{2,10},{10,18},{18,26},{... | collective-permute-start | bytes 516104 | tf_op jit(solution)/shard_map/ppermute | solution.py:14
  94.6 2.6 %collective-permute-done = bf16[24,3584]{1,0:T(8,128)(2,1)S(1)} collective-permute-done((bf16[24,3584]{1,0:T(8,128)(2,1)}, bf16[24,3584]{1,0:T(8,128)(2,1)S(1)}, u32[]{:S(2)}, u32[]{:S(2)}) %collective-permute-start) | collective-permute-done | bytes 172064 | tf_op jit(solution)/shard_map/ppermute | solution.py:14
  99.0 1.7 %broadcast_in_dim.30 = bf16[4,2,7,3584]{3,2,1,0:T(8,128)(2,1)} broadcast(bf16[4,7,3584]{2,1,0:T(8,128)(2,1)} %reshape.180), dimensions={0,2,3} | broadcast | bytes 602112 | tf_op jit(solution)/shard_map/broadcast_in_dim | solution.py:36
  100.7 3.8 %all-to-all-start.7 = ((bf16[8,7,3584]{2,1,0:T(8,128)(2,1)}), bf16[8,7,3584]{2,1,0:T(8,128)(2,1)S(1)}, u32[]{:S(2)}, u32[]{:S(2)}) async-start(bf16[8,7,3584]{2,1,0:T(8,128)(2,1)} %bitcast.133), calls=%async_computation.7 | async-start | bytes 917504 | tf_op jit(solution)/shard_map/all_to_all | solution.py:95
  104.5 1.9 %fusion.20 = f32[8,7,128]{2,1,0:T(8,128)} fusion(bf16[8,7,3584]{2,1,0:T(8,128)(2,1)} %all-to-all-done.8, bf16[1,3584,128]{2,1,0:T(8,128)(2,1)S(1)} %copy-done.1), kind=kOutput, calls=%fused_computation.38 | convolution fusion | flops 51380224 | bytes 1347584 | tf_op jit(solution)/shard_map/scd,dh->sch/dot_general | solution.py:96
  106.5 2.0 %fusion.9 = f32[8,7,128]{2,1,0:T(8,128)} fusion(bf16[8,7,3584]{2,1,0:T(8,128)(2,1)} %all-to-all-done.8, bf16[1,3584,128]{2,1,0:T(8,128)(2,1)S(1)} %copy-done), kind=kOutput, calls=%fused_computation.27 | convolution fusion | flops 51380224 | bytes 1347584 | tf_op jit(solution)/shard_map/scd,dh->sch/dot_general | solution.py:99
  108.4 5.1 %all-to-all-done.7 = bf16[8,7,3584]{2,1,0:T(8,128)(2,1)S(1)} async-done(((bf16[8,7,3584]{2,1,0:T(8,128)(2,1)}), bf16[8,7,3584]{2,1,0:T(8,128)(2,1)S(1)}, u32[]{:S(2)}, u32[]{:S(2)}) %all-to-all-start.7) | async-done | bytes 401440 | tf_op jit(solution)/shard_map/all_to_all | solution.py:95
  113.5 1.9 %broadcast_in_dim.26 = bf16[4,2,7,3584]{3,2,1,0:T(8,128)(2,1)} broadcast(bf16[4,7,3584]{2,1,0:T(8,128)(2,1)} %reshape.172), dimensions={0,2,3} | broadcast | bytes 602112 | tf_op jit(solution)/shard_map/broadcast_in_dim | solution.py:36
  115.5 3.5 %all-to-all-start.2 = ((bf16[8,7,3584]{2,1,0:T(8,128)(2,1)}), bf16[8,7,3584]{2,1,0:T(8,128)(2,1)S(1)}, u32[]{:S(2)}, u32[]{:S(2)}) async-start(bf16[8,7,3584]{2,1,0:T(8,128)(2,1)} %bitcast.132), calls=%async_computation.2 | async-start | bytes 917504 | tf_op jit(solution)/shard_map/all_to_all | solution.py:80
  119.0 1.5 fusion.2
  122.2 5.6 %all-to-all-done.2 = bf16[8,7,3584]{2,1,0:T(8,128)(2,1)S(1)} async-done(((bf16[8,7,3584]{2,1,0:T(8,128)(2,1)}), bf16[8,7,3584]{2,1,0:T(8,128)(2,1)S(1)}, u32[]{:S(2)}, u32[]{:S(2)}) %all-to-all-start.2) | async-done | bytes 401440 | tf_op jit(solution)/shard_map/all_to_all | solution.py:80
  127.9 4.1 %all-to-all-start.9 = ((bf16[8,7,3584]{2,1,0:T(8,128)(2,1)}), bf16[8,7,3584]{2,1,0:T(8,128)(2,1)}, u32[]{:S(2)}, u32[]{:S(2)}) async-start(bf16[8,7,3584]{2,1,0:T(8,128)(2,1)} %copy.44), calls=%async_computation.9 | async-start | bytes 917504 | tf_op jit(solution)/shard_map/all_to_all | solution.py:111
  133.8 7.2 %all-to-all-done.9 = bf16[8,7,3584]{2,1,0:T(8,128)(2,1)} async-done(((bf16[8,7,3584]{2,1,0:T(8,128)(2,1)}), bf16[8,7,3584]{2,1,0:T(8,128)(2,1)}, u32[]{:S(2)}, u32[]{:S(2)}) %all-to-all-start.9) | async-done | bytes 401440 | tf_op jit(solution)/shard_map/all_to_all | solution.py:111
  141.0 3.5 %all-to-all-start.3 = ((bf16[8,7,3584]{2,1,0:T(8,128)(2,1)}), bf16[8,7,3584]{2,1,0:T(8,128)(2,1)S(1)}, u32[]{:S(2)}, u32[]{:S(2)}) async-start(bf16[8,7,3584]{2,1,0:T(8,128)(2,1)} %copy.32), calls=%async_computation.3 | async-start | bytes 917504 | tf_op jit(solution)/shard_map/all_to_all | solution.py:93
  147.5 5.9 %all-to-all-done.3 = bf16[8,7,3584]{2,1,0:T(8,128)(2,1)S(1)} async-done(((bf16[8,7,3584]{2,1,0:T(8,128)(2,1)}), bf16[8,7,3584]{2,1,0:T(8,128)(2,1)S(1)}, u32[]{:S(2)}, u32[]{:S(2)}) %all-to-all-start.3) | async-done | bytes 401440 | tf_op jit(solution)/shard_map/all_to_all | solution.py:93
  155.1 1.8 %fusion.60 = bf16[1,24,3584]{2,1,0:T(8,128)(2,1)} fusion(f32[24,3584]{1,0:T(8,128)S(1)} %gather_fusion.3, bf16[24,3584]{1,0:T(8,128)(2,1)} %collective-permute-done.1, f32[24]{0:T(128)S(1)} %broadcast_multiply_fusion, f32[24]{0:T(128)S(1)} %copy-done.40, f32[24]{0:T(128)S(1)} %copy-done.32, f32[3584]{0:T(1024)S(1)} %copy-done.13, ...), kind=kLoop, calls=%fused_computation.95 | loop fusion | flops 860160 | bytes 874808 | tf_op jit(solution)/shard_map/broadcast_in_dim | solution.py:124
  (164 shorter events, 42.1 us)
Async XLA Ops:
  0.6 25.2 %copy-start = (bf16[1,3584,128]{2,1,0:T(8,128)(2,1)S(1)}, bf16[1,3584,128]{2,1,0:T(8,128)(2,1)}, u32[]{:S(2)}) copy-start(bf16[1,3584,128]{2,1,0:T(8,128)(2,1)} %param.21) | copy-start | bytes 2752516
  3.3 1.5 copy-start.29
  3.3 1.4 copy-start.18
  4.7 9.3 %copy-start.19 = (s32[24]{0:T(128)}, s32[24]{0:T(128)S(1)}, u32[]{:S(2)}) copy-start(s32[24]{0:T(128)S(1)} %get-tuple-element.6) | copy-start | bytes 292
  4.7 11.2 %copy-start.10 = (f32[3584]{0:T(1024)}, f32[3584]{0:T(1024)S(1)}, u32[]{:S(2)}) copy-start(f32[3584]{0:T(1024)S(1)} %reduce) | copy-start | bytes 43012
  6.8 8.1 %copy-start.9 = (bf16[1,24,3584]{2,1,0:T(8,128)(2,1)S(1)}, bf16[1,24,3584]{2,1,0:T(8,128)(2,1)}, u32[]{:S(2)}) copy-start(bf16[1,24,3584]{2,1,0:T(8,128)(2,1)} %param.13) | copy-start | bytes 516100
  6.8 14.3 %all-to-all-start.5 = ((bf16[8,7,3584]{2,1,0:T(8,128)(2,1)}), bf16[8,7,3584]{2,1,0:T(8,128)(2,1)S(1)}, u32[]{:S(2)}, u32[]{:S(2)}) async-start(bf16[8,7,3584]{2,1,0:T(8,128)(2,1)} %bitcast.24), calls=%async_computation.5 | async-start | bytes 917504 | tf_op jit(solution)/shard_map/all_to_all | solution.py:94
  17.9 7.6 %copy-start.1 = (bf16[1,3584,128]{2,1,0:T(8,128)(2,1)S(1)}, bf16[1,3584,128]{2,1,0:T(8,128)(2,1)}, u32[]{:S(2)}) copy-start(bf16[1,3584,128]{2,1,0:T(8,128)(2,1)} %param.20) | copy-start | bytes 2752516
  22.0 12.4 %all-to-all-start.4 = ((bf16[8,7,3584]{2,1,0:T(8,128)(2,1)}), bf16[8,7,3584]{2,1,0:T(8,128)(2,1)S(1)}, u32[]{:S(2)}, u32[]{:S(2)}) async-start(bf16[8,7,3584]{2,1,0:T(8,128)(2,1)} %bitcast.22), calls=%async_computation.4 | async-start | bytes 917504 | tf_op jit(solution)/shard_map/all_to_all | solution.py:95
  26.1 12.7 %copy-start.2 = (bf16[1,128,3584]{2,1,0:T(8,128)(2,1)S(1)}, bf16[1,128,3584]{2,1,0:T(8,128)(2,1)}, u32[]{:S(2)}) copy-start(bf16[1,128,3584]{2,1,0:T(8,128)(2,1)} %param.22) | copy-start | bytes 2752516
  35.3 12.4 %all-to-all-start = ((bf16[8,7,3584]{2,1,0:T(8,128)(2,1)}), bf16[8,7,3584]{2,1,0:T(8,128)(2,1)S(1)}, u32[]{:S(2)}, u32[]{:S(2)}) async-start(bf16[8,7,3584]{2,1,0:T(8,128)(2,1)} %bitcast.131), calls=%async_computation | async-start | bytes 917504 | tf_op jit(solution)/shard_map/all_to_all | solution.py:80
  47.8 13.2 %all-to-all-start.6 = ((bf16[8,7,3584]{2,1,0:T(8,128)(2,1)}), bf16[8,7,3584]{2,1,0:T(8,128)(2,1)}, u32[]{:S(2)}, u32[]{:S(2)}) async-start(bf16[8,7,3584]{2,1,0:T(8,128)(2,1)} %copy.38), calls=%async_computation.6 | async-start | bytes 917504 | tf_op jit(solution)/shard_map/all_to_all | solution.py:111
  60.9 15.1 %all-to-all-start.1 = ((bf16[8,7,3584]{2,1,0:T(8,128)(2,1)}), bf16[8,7,3584]{2,1,0:T(8,128)(2,1)}, u32[]{:S(2)}, u32[]{:S(2)}) async-start(bf16[8,7,3584]{2,1,0:T(8,128)(2,1)} %copy.27), calls=%async_computation.1 | async-start | bytes 917504 | tf_op jit(solution)/shard_map/all_to_all | solution.py:93
  68.0 1.7 %copy-start.3 = (bf16[1,2,24,3584]{3,2,1,0:T(8,128)(2,1)S(1)}, bf16[1,2,24,3584]{3,2,1,0:T(8,128)(2,1)}, u32[]{:S(2)}) copy-start(bf16[1,2,24,3584]{3,2,1,0:T(8,128)(2,1)} %param.15) | copy-start | bytes 1032196
  70.3 1.3 copy-start.4
  70.3 1.3 copy-start.11
  70.3 1.3 copy-start.15
  73.1 19.5 %collective-permute-start.1 = (bf16[24,3584]{1,0:T(8,128)(2,1)}, bf16[24,3584]{1,0:T(8,128)(2,1)}, u32[]{:S(2)}, u32[]{:S(2)}) collective-permute-start(bf16[24,3584]{1,0:T(8,128)(2,1)} %fusion.33), channel_id=1, source_target_pairs={{8,0},{16,8},{24,16},{9,1},{17,9},{25,17},{10,2},{18,10},{26,18},{... | collective-permute-start | bytes 516104 | tf_op jit(solution)/shard_map/ppermute | solution.py:14
  76.8 22.2 %all-to-all-start.8 = ((bf16[8,7,3584]{2,1,0:T(8,128)(2,1)}), bf16[8,7,3584]{2,1,0:T(8,128)(2,1)}, u32[]{:S(2)}, u32[]{:S(2)}) async-start(bf16[8,7,3584]{2,1,0:T(8,128)(2,1)} %bitcast.31), calls=%async_computation.8 | async-start | bytes 917504 | tf_op jit(solution)/shard_map/all_to_all | solution.py:94
  88.0 4.7 %copy-start.21 = (s32[24]{0:T(128)S(1)}, s32[24]{0:T(128)}, u32[]{:S(2)}) copy-start(s32[24]{0:T(128)} %copy-done.19) | copy-start | bytes 292
  88.0 4.7 %copy-start.26 = (f32[24]{0:T(128)S(1)}, f32[24]{0:T(128)}, u32[]{:S(2)}) copy-start(f32[24]{0:T(128)} %get-tuple-element.13) | copy-start | bytes 292
  88.0 9.2 %collective-permute-start = (bf16[24,3584]{1,0:T(8,128)(2,1)}, bf16[24,3584]{1,0:T(8,128)(2,1)S(1)}, u32[]{:S(2)}, u32[]{:S(2)}) collective-permute-start(bf16[24,3584]{1,0:T(8,128)(2,1)} %fusion.41), channel_id=1, source_target_pairs={{0,8},{8,16},{16,24},{1,9},{9,17},{17,25},{2,10},{10,18},{18,26},{... | collective-permute-start | bytes 516104 | tf_op jit(solution)/shard_map/ppermute | solution.py:14
  94.6 2.7 %copy-start.12 = (f32[3584]{0:T(1024)S(1)}, f32[3584]{0:T(1024)}, u32[]{:S(2)}) copy-start(f32[3584]{0:T(1024)} %copy-done.10) | copy-start | bytes 43012
  97.2 1.0 copy-start.7
  100.7 12.8 %all-to-all-start.7 = ((bf16[8,7,3584]{2,1,0:T(8,128)(2,1)}), bf16[8,7,3584]{2,1,0:T(8,128)(2,1)S(1)}, u32[]{:S(2)}, u32[]{:S(2)}) async-start(bf16[8,7,3584]{2,1,0:T(8,128)(2,1)} %bitcast.133), calls=%async_computation.7 | async-start | bytes 917504 | tf_op jit(solution)/shard_map/all_to_all | solution.py:95
  113.5 1.9 %copy-start.6 = (bf16[8,7,3584]{2,1,0:T(8,128)(2,1)}, bf16[8,7,3584]{2,1,0:T(8,128)(2,1)S(1)}, u32[]{:S(2)}) copy-start(bf16[8,7,3584]{2,1,0:T(8,128)(2,1)S(1)} %all-to-all-done.7) | copy-start | bytes 1204228
  115.5 12.4 %all-to-all-start.2 = ((bf16[8,7,3584]{2,1,0:T(8,128)(2,1)}), bf16[8,7,3584]{2,1,0:T(8,128)(2,1)S(1)}, u32[]{:S(2)}, u32[]{:S(2)}) async-start(bf16[8,7,3584]{2,1,0:T(8,128)(2,1)} %bitcast.132), calls=%async_computation.2 | async-start | bytes 917504 | tf_op jit(solution)/shard_map/all_to_all | solution.py:80
  118.9 1.5 copy-start.16
  118.9 1.5 copy-start.17
  127.9 13.2 %all-to-all-start.9 = ((bf16[8,7,3584]{2,1,0:T(8,128)(2,1)}), bf16[8,7,3584]{2,1,0:T(8,128)(2,1)}, u32[]{:S(2)}, u32[]{:S(2)}) async-start(bf16[8,7,3584]{2,1,0:T(8,128)(2,1)} %copy.44), calls=%async_computation.9 | async-start | bytes 917504 | tf_op jit(solution)/shard_map/all_to_all | solution.py:111
  141.0 12.4 %all-to-all-start.3 = ((bf16[8,7,3584]{2,1,0:T(8,128)(2,1)}), bf16[8,7,3584]{2,1,0:T(8,128)(2,1)S(1)}, u32[]{:S(2)}, u32[]{:S(2)}) async-start(bf16[8,7,3584]{2,1,0:T(8,128)(2,1)} %copy.32), calls=%async_computation.3 | async-start | bytes 917504 | tf_op jit(solution)/shard_map/all_to_all | solution.py:93
  155.1 1.8 %copy-start.8 = (bf16[24,3584]{1,0:T(8,128)(2,1)S(1)}, bf16[24,3584]{1,0:T(8,128)(2,1)}, u32[]{:S(2)}) copy-start(bf16[24,3584]{1,0:T(8,128)(2,1)} %copy-done.7) | copy-start | bytes 516100
  (21 other events, 14.2 us)
where the time goes:
time: 160 us; the launch traced here: 158 us
  waiting for transfers between devices  49.7 us (31%)
  starting transfers between devices  45.5 us (28%)
  local copies, waits for them, and re-layouts  28.6 us (18%)
  other arithmetic  18.8 us (12%)
  matrix products  14.5 us (9%)
    all_to_all x2, waiting for transfers between devices, local(): lax.all_to_all(bwd_partial, 'expert', split_axis=0, concat_axis=0, tiled=...  14.4 us
    all_to_all x2, waiting for transfers between devices, local(): lax.all_to_all(bwd_grads, 'expert', split_axis=0, concat_axis=0, tiled=True)  13.4 us
    all_to_all x2, waiting for transfers between devices, local(): lax.all_to_all(fwd_slots, 'expert', split_axis=0, concat_axis=0, tiled=True)  11.3 us
    all_to_all x2, starting transfers between devices, local(): lax.all_to_all(bwd_inputs, 'expert', split_axis=0, concat_axis=0, tiled=T...  9.46 us
    all_to_all x2, starting transfers between devices, local(): lax.all_to_all(bwd_partial, 'expert', split_axis=0, concat_axis=0, tiled=...  8.24 us
    all_to_all x2, starting transfers between devices, local(): lax.all_to_all(fwd_partial, 'expert', split_axis=0, concat_axis=0, tiled=...  7.59 us
    all_to_all x2, starting transfers between devices, local(): lax.all_to_all(bwd_grads, 'expert', split_axis=0, concat_axis=0, tiled=True)  7.28 us
    unnamed x82, local copies, waits for them, and re-layouts  7.25 us
  transfers between devices with their start and end apart: 12, of which 9 were waited for; matrix products, arithmetic and copies ran while one was open for 26% of the time, Pallas kernels for 0%

commit v1 on v0

--- a/solution.py
+++ b/solution.py
@@ -6,6 +6,22 @@
 EXPERTS = 4
 CAP = 7
 EPS = 1e-06
+
+
+def exchange_in_pairs(x, axis, split, join):
+    ways, here = (lax.axis_size(axis), lax.axis_index(axis))
+    width = x.shape[split] // ways
+    lengths = list(x.shape)
+    lengths[split] = width
+    height = lengths[join]
+    lengths[join] = height * ways
+    full = jnp.zeros(lengths, x.dtype)
+    for mask in range(ways):
+        part = lax.dynamic_slice_in_dim(x, (here ^ mask) * width, width, axis=split)
+        if mask:
+            part = lax.ppermute(part, axis, [(d, d ^ mask) for d in range(ways)])
+        full = lax.dynamic_update_slice_in_dim(full, part, (here ^ mask) * height, axis=join)
+    return full
 
 
 def passed_along(array, axis, by):
@@ -108,7 +124,7 @@
             "sch,dh->scd", dup, up_cols, preferred_element_type=jnp.float32
         )
         bwd_partial = result.astype(jnp.bfloat16)
-        bwd_back = lax.all_to_all(bwd_partial, "expert", split_axis=0, concat_axis=0, tiled=True)
+        bwd_back = exchange_in_pairs(bwd_partial, "expert", 0, 0)
         moe_rows = collect_rows(fwd_back, fwd_index, shards)
         new_forward = (fwd_raw + fwd_gate[0, moment][:, None] * moe_rows).astype(jnp.bfloat16)
         dnorm = collect_rows(bwd_back, bwd_index, shards)

time: 160 us -> 201 us (1.26); the launches traced: 158 us -> 197 us
  local copies, waits for them, and re-layouts: 28.6 us -> 78.4 us
  waiting for transfers between devices: 49.7 us -> 28.6 us
  other arithmetic: 18.8 us -> 23.4 us
  starting transfers between devices: 45.5 us -> 48.7 us
  matrix products: 14.5 us -> 16.8 us
    dynamic_update_slice x0 -> x16, local copies, waits for them, and re-layouts: none -> 42.7 us  [exchange_in_pairs(): lax.dynamic_update_slice_in_dim(full, part, (here ^ mask) * height, axis=...]
    all_to_all x2 -> x0, waiting for transfers between devices: 14.4 us -> none  [local(): lax.all_to_all(bwd_partial, 'expert', split_axis=0, concat_axis=0, tiled=...]
    ppermute x0 -> x14, starting transfers between devices: none -> 10.2 us  [exchange_in_pairs(): part = lax.ppermute(part, axis, [(d, d ^ mask) for d in range(ways)])]
    all_to_all x2, waiting for transfers between devices: 11.3 us -> 1.26 us  [local(): lax.all_to_all(fwd_slots, 'expert', split_axis=0, concat_axis=0, tiled=True)]
    all_to_all x2 -> x0, starting transfers between devices: 8.24 us -> none  [local(): lax.all_to_all(bwd_partial, 'expert', split_axis=0, concat_axis=0, tiled=...]
    ppermute x2, waiting for transfers between devices: 2.57 us -> 6.04 us  [passed_along(): return lax.ppermute(array, axis, pairs)]
    dynamic_slice x0 -> x2, local copies, waits for them, and re-layouts: none -> 3.19 us  [exchange_in_pairs(): part = lax.dynamic_slice_in_dim(x, (here ^ mask) * width, width, axis=split)]
    all_to_all x2, waiting for transfers between devices: 13.4 us -> 10.5 us  [local(): lax.all_to_all(bwd_grads, 'expert', split_axis=0, concat_axis=0, tiled=True)]
  transfers between devices with their start and end apart: 12 -> 24, of which waited for: 9 -> 7; matrix products, arithmetic and copies ran while one was open for 26% -> 47% of each run, Pallas kernels for 0% -> 0%
where the time goes in v1:
time: 201 us; the launch traced here: 197 us
  local copies, waits for them, and re-layouts  78.4 us (39%)
  starting transfers between devices  48.7 us (24%)
  waiting for transfers between devices  28.6 us (14%)
  other arithmetic  23.4 us (12%)
  matrix products  16.8 us (8%)
    dynamic_update_slice x16, local copies, waits for them, and re-layouts, exchange_in_pairs(): lax.dynamic_update_slice_in_dim(full, part, (here ^ mask) * height, axis=...  42.7 us
    all_to_all x2, waiting for transfers between devices, local(): lax.all_to_all(bwd_grads, 'expert', split_axis=0, concat_axis=0, tiled=True)  10.5 us
    ppermute x14, starting transfers between devices, exchange_in_pairs(): part = lax.ppermute(part, axis, [(d, d ^ mask) for d in range(ways)])  10.2 us
    all_to_all x2, starting transfers between devices, local(): lax.all_to_all(bwd_inputs, 'expert', split_axis=0, concat_axis=0, tiled=T...  9.63 us
    all_to_all x2, starting transfers between devices, local(): lax.all_to_all(fwd_partial, 'expert', split_axis=0, concat_axis=0, tiled=...  8.35 us
    all_to_all x2, starting transfers between devices, local(): lax.all_to_all(fwd_slots, 'expert', split_axis=0, concat_axis=0, tiled=True)  7.6 us
    all_to_all x2, starting transfers between devices, local(): lax.all_to_all(bwd_grads, 'expert', split_axis=0, concat_axis=0, tiled=True)  7.39 us
    unnamed x90, local copies, waits for them, and re-layouts  6.98 us
  transfers between devices with their start and end apart: 24, of which 7 were waited for; matrix products, arithmetic and copies ran while one was open for 47% of the time, Pallas kernels for 0%

profile of v1, /device:TPU:0, one launch (start us, length us, event | category | flops | bytes accessed | tf_op | source)
XLA Modules:
  0.0 197.2 jit_solution(1070955018933358831)
XLA Ops:
  7.5 5.3 %all-to-all-start.5 = ((bf16[8,7,3584]{2,1,0:T(8,128)(2,1)}), bf16[8,7,3584]{2,1,0:T(8,128)(2,1)S(1)}, u32[]{:S(2)}, u32[]{:S(2)}) async-start(bf16[8,7,3584]{2,1,0:T(8,128)(2,1)} %bitcast.24), calls=%async_computation.5 | async-start | bytes 917504 | tf_op jit(solution)/shard_map/all_to_all | solution.py:110
  19.3 2.6 %all-to-all-done.5 = bf16[8,7,3584]{2,1,0:T(8,128)(2,1)S(1)} async-done(((bf16[8,7,3584]{2,1,0:T(8,128)(2,1)}), bf16[8,7,3584]{2,1,0:T(8,128)(2,1)S(1)}, u32[]{:S(2)}, u32[]{:S(2)}) %all-to-all-start.5) | async-done | bytes 401440 | tf_op jit(solution)/shard_map/all_to_all | solution.py:110
  22.6 3.5 %all-to-all-start.4 = ((bf16[8,7,3584]{2,1,0:T(8,128)(2,1)}), bf16[8,7,3584]{2,1,0:T(8,128)(2,1)S(1)}, u32[]{:S(2)}, u32[]{:S(2)}) async-start(bf16[8,7,3584]{2,1,0:T(8,128)(2,1)} %bitcast.22), calls=%async_computation.4 | async-start | bytes 917504 | tf_op jit(solution)/shard_map/all_to_all | solution.py:111
  28.0 7.0 %all-to-all-done.4 = bf16[8,7,3584]{2,1,0:T(8,128)(2,1)S(1)} async-done(((bf16[8,7,3584]{2,1,0:T(8,128)(2,1)}), bf16[8,7,3584]{2,1,0:T(8,128)(2,1)S(1)}, u32[]{:S(2)}, u32[]{:S(2)}) %all-to-all-start.4) | async-done | bytes 401440 | tf_op jit(solution)/shard_map/all_to_all | solution.py:111
  37.0 3.5 %all-to-all-start = ((bf16[8,7,3584]{2,1,0:T(8,128)(2,1)}), bf16[8,7,3584]{2,1,0:T(8,128)(2,1)S(1)}, u32[]{:S(2)}, u32[]{:S(2)}) async-start(bf16[8,7,3584]{2,1,0:T(8,128)(2,1)} %bitcast.129), calls=%async_computation | async-start | bytes 917504 | tf_op jit(solution)/shard_map/all_to_all | solution.py:96
  53.3 4.1 %all-to-all-start.1 = ((bf16[8,7,3584]{2,1,0:T(8,128)(2,1)}), bf16[8,7,3584]{2,1,0:T(8,128)(2,1)}, u32[]{:S(2)}, u32[]{:S(2)}) async-start(bf16[8,7,3584]{2,1,0:T(8,128)(2,1)} %copy.27), calls=%async_computation.1 | async-start | bytes 917504 | tf_op jit(solution)/shard_map/all_to_all | solution.py:109
  57.4 2.7 %dynamic_update_slice.48 = bf16[8,7,3584]{2,0,1:T(8,128)(2,1)S(1)} dynamic-update-slice(bf16[8,7,3584]{2,0,1:T(8,128)(2,1)S(1)} %broadcast.123.clone, bf16[1,7,3584]{2,0,1:T(2,128)(2,1)} %get-tuple-element.28, s32[]{:T(128)S(6)} %select_n.23, s32[]{:T(128)} %constant.24.clone.1, s32[]{:T(128)} %constant.24.clone.1) | dynamic-update-slice | bytes 100356 | tf_op jit(solution)/shard_map/dynamic_update_slice | solution.py:23
  60.1 2.7 %dynamic_update_slice.49 = bf16[8,7,3584]{2,0,1:T(8,128)(2,1)S(1)} dynamic-update-slice(bf16[8,7,3584]{2,0,1:T(8,128)(2,1)S(1)} %dynamic_update_slice.48, bf16[1,7,3584]{2,0,1:T(2,128)(2,1)} %collective-permute-done.1, s32[]{:T(128)S(6)} %select_n.24, s32[]{:T(128)} %constant.24.clone.1, s32[]{:T(128)} %constant.24.clone.1) | dynamic-update-slice | bytes 100356 | tf_op jit(solution)/shard_map/dynamic_update_slice | solution.py:23
  62.8 2.7 %dynamic_update_slice.50 = bf16[8,7,3584]{2,0,1:T(8,128)(2,1)S(1)} dynamic-update-slice(bf16[8,7,3584]{2,0,1:T(8,128)(2,1)S(1)} %dynamic_update_slice.49, bf16[1,7,3584]{2,0,1:T(2,128)(2,1)} %collective-permute-done.2, s32[]{:T(128)S(6)} %select_n.25, s32[]{:T(128)} %constant.24.clone.1, s32[]{:T(128)} %constant.24.clone.1) | dynamic-update-slice | bytes 100356 | tf_op jit(solution)/shard_map/dynamic_update_slice | solution.py:23
  65.5 2.7 %dynamic_update_slice.51 = bf16[8,7,3584]{2,0,1:T(8,128)(2,1)S(1)} dynamic-update-slice(bf16[8,7,3584]{2,0,1:T(8,128)(2,1)S(1)} %dynamic_update_slice.50, bf16[1,7,3584]{2,0,1:T(2,128)(2,1)} %collective-permute-done.3, s32[]{:T(128)S(6)} %select_n.26, s32[]{:T(128)} %constant.24.clone.1, s32[]{:T(128)} %constant.24.clone.1) | dynamic-update-slice | bytes 100356 | tf_op jit(solution)/shard_map/dynamic_update_slice | solution.py:23
  68.1 2.7 %dynamic_update_slice.52 = bf16[8,7,3584]{2,0,1:T(8,128)(2,1)S(1)} dynamic-update-slice(bf16[8,7,3584]{2,0,1:T(8,128)(2,1)S(1)} %dynamic_update_slice.51, bf16[1,7,3584]{2,0,1:T(2,128)(2,1)} %collective-permute-done.4, s32[]{:T(128)S(6)} %select_n.27, s32[]{:T(128)} %constant.24.clone.1, s32[]{:T(128)} %constant.24.clone.1) | dynamic-update-slice | bytes 100356 | tf_op jit(solution)/shard_map/dynamic_update_slice | solution.py:23
  70.8 2.7 %dynamic_update_slice.53 = bf16[8,7,3584]{2,0,1:T(8,128)(2,1)S(1)} dynamic-update-slice(bf16[8,7,3584]{2,0,1:T(8,128)(2,1)S(1)} %dynamic_update_slice.52, bf16[1,7,3584]{2,0,1:T(2,128)(2,1)} %collective-permute-done.5, s32[]{:T(128)S(6)} %select_n.28, s32[]{:T(128)} %constant.24.clone.1, s32[]{:T(128)} %constant.24.clone.1) | dynamic-update-slice | bytes 100356 | tf_op jit(solution)/shard_map/dynamic_update_slice | solution.py:23
  73.5 2.7 %dynamic_update_slice.54 = bf16[8,7,3584]{2,0,1:T(8,128)(2,1)S(1)} dynamic-update-slice(bf16[8,7,3584]{2,0,1:T(8,128)(2,1)S(1)} %dynamic_update_slice.53, bf16[1,7,3584]{2,0,1:T(2,128)(2,1)} %collective-permute-done.6, s32[]{:T(128)S(6)} %select_n.29, s32[]{:T(128)} %constant.24.clone.1, s32[]{:T(128)} %constant.24.clone.1) | dynamic-update-slice | bytes 100356 | tf_op jit(solution)/shard_map/dynamic_update_slice | solution.py:23
  76.2 2.7 %dynamic_update_slice.55 = bf16[8,7,3584]{2,0,1:T(8,128)(2,1)S(1)} dynamic-update-slice(bf16[8,7,3584]{2,0,1:T(8,128)(2,1)S(1)} %dynamic_update_slice.54, bf16[1,7,3584]{2,0,1:T(2,128)(2,1)} %collective-permute-done.7, s32[]{:T(128)S(6)} %select_n.30, s32[]{:T(128)} %constant.24.clone.1, s32[]{:T(128)} %constant.24.clone.1) | dynamic-update-slice | bytes 100356 | tf_op jit(solution)/shard_map/dynamic_update_slice | solution.py:23
  80.3 2.2 %reduce_sum.134 = f32[4,7,3584]{2,0,1:T(4,128)S(1)} reduce(f32[4,2,7,3584]{3,1,0,2:T(2,128)} %reshape.190, f32[]{:T(128)} %constant.21.clone.1), dimensions={1}, to_apply=%region_11.13 | reduce | flops 100352 | bytes 1204228 | tf_op jit(solution)/shard_map/reduce_sum | solution.py:58
  92.3 6.0 %collective-permute-done.8 = bf16[24,3584]{1,0:T(8,128)(2,1)} collective-permute-done((bf16[24,3584]{1,0:T(8,128)(2,1)}, bf16[24,3584]{1,0:T(8,128)(2,1)}, u32[]{:S(2)}, u32[]{:S(2)}) %collective-permute-start.8) | collective-permute-done | bytes 172064 | tf_op jit(solution)/shard_map/ppermute | solution.py:30
  101.1 4.3 %all-to-all-start.7 = ((bf16[8,7,3584]{2,1,0:T(8,128)(2,1)}), bf16[8,7,3584]{2,1,0:T(8,128)(2,1)}, u32[]{:S(2)}, u32[]{:S(2)}) async-start(bf16[8,7,3584]{2,1,0:T(8,128)(2,1)} %bitcast.30), calls=%async_computation.7 | async-start | bytes 917504 | tf_op jit(solution)/shard_map/all_to_all | solution.py:110
  112.5 4.1 %collective-permute-start = (bf16[24,3584]{1,0:T(8,128)(2,1)}, bf16[24,3584]{1,0:T(8,128)(2,1)}, u32[]{:S(2)}, u32[]{:S(2)}) collective-permute-start(bf16[24,3584]{1,0:T(8,128)(2,1)} %fusion.41), channel_id=1, source_target_pairs={{0,8},{8,16},{16,24},{1,9},{9,17},{17,25},{2,10},{10,18},{18,26},{... | collective-permute-start | bytes 516104 | tf_op jit(solution)/shard_map/ppermute | solution.py:30
  117.4 3.9 %all-to-all-start.6 = ((bf16[8,7,3584]{2,1,0:T(8,128)(2,1)}), bf16[8,7,3584]{2,1,0:T(8,128)(2,1)S(1)}, u32[]{:S(2)}, u32[]{:S(2)}) async-start(bf16[8,7,3584]{2,1,0:T(8,128)(2,1)} %bitcast.130), calls=%async_computation.6 | async-start | bytes 917504 | tf_op jit(solution)/shard_map/all_to_all | solution.py:111
  126.9 3.5 %all-to-all-done.6 = bf16[8,7,3584]{2,1,0:T(8,128)(2,1)S(1)} async-done(((bf16[8,7,3584]{2,1,0:T(8,128)(2,1)}), bf16[8,7,3584]{2,1,0:T(8,128)(2,1)S(1)}, u32[]{:S(2)}, u32[]{:S(2)}) %all-to-all-start.6) | async-done | bytes 401440 | tf_op jit(solution)/shard_map/all_to_all | solution.py:111
  142.1 4.1 %all-to-all-start.2 = ((bf16[8,7,3584]{2,1,0:T(8,128)(2,1)}), bf16[8,7,3584]{2,1,0:T(8,128)(2,1)}, u32[]{:S(2)}, u32[]{:S(2)}) async-start(bf16[8,7,3584]{2,1,0:T(8,128)(2,1)} %bitcast.14), calls=%async_computation.2 | async-start | bytes 917504 | tf_op jit(solution)/shard_map/all_to_all | solution.py:96
  146.2 2.7 %dynamic_update_slice.56 = bf16[8,7,3584]{2,0,1:T(8,128)(2,1)S(1)} dynamic-update-slice(bf16[8,7,3584]{2,0,1:T(8,128)(2,1)S(1)} %broadcast.123, bf16[1,7,3584]{2,0,1:T(2,128)(2,1)} %get-tuple-element.20, s32[]{:T(128)S(6)} %select_n.23, s32[]{:T(128)} %constant.24.clone.1, s32[]{:T(128)} %constant.24.clone.1) | dynamic-update-slice | bytes 100356 | tf_op jit(solution)/shard_map/dynamic_update_slice | solution.py:23
  148.9 2.7 %dynamic_update_slice.57 = bf16[8,7,3584]{2,0,1:T(8,128)(2,1)S(1)} dynamic-update-slice(bf16[8,7,3584]{2,0,1:T(8,128)(2,1)S(1)} %dynamic_update_slice.56, bf16[1,7,3584]{2,0,1:T(2,128)(2,1)} %copy-done.19, s32[]{:T(128)S(6)} %select_n.24, s32[]{:T(128)} %constant.24.clone.1, s32[]{:T(128)} %constant.24.clone.1) | dynamic-update-slice | bytes 100356 | tf_op jit(solution)/shard_map/dynamic_update_slice | solution.py:23
  151.6 2.7 %dynamic_update_slice.58 = bf16[8,7,3584]{2,0,1:T(8,128)(2,1)S(1)} dynamic-update-slice(bf16[8,7,3584]{2,0,1:T(8,128)(2,1)S(1)} %dynamic_update_slice.57, bf16[1,7,3584]{2,0,1:T(2,128)(2,1)} %copy-done.20, s32[]{:T(128)S(6)} %select_n.25, s32[]{:T(128)} %constant.24.clone.1, s32[]{:T(128)} %constant.24.clone.1) | dynamic-update-slice | bytes 100356 | tf_op jit(solution)/shard_map/dynamic_update_slice | solution.py:23
  154.3 2.7 %dynamic_update_slice.59 = bf16[8,7,3584]{2,0,1:T(8,128)(2,1)S(1)} dynamic-update-slice(bf16[8,7,3584]{2,0,1:T(8,128)(2,1)S(1)} %dynamic_update_slice.58, bf16[1,7,3584]{2,0,1:T(2,128)(2,1)} %collective-permute-done.11, s32[]{:T(128)S(6)} %select_n.26, s32[]{:T(128)} %constant.24.clone.1, s32[]{:T(128)} %constant.24.clone.1) | dynamic-update-slice | bytes 100356 | tf_op jit(solution)/shard_map/dynamic_update_slice | solution.py:23
  157.0 2.7 %dynamic_update_slice.60 = bf16[8,7,3584]{2,0,1:T(8,128)(2,1)S(1)} dynamic-update-slice(bf16[8,7,3584]{2,0,1:T(8,128)(2,1)S(1)} %dynamic_update_slice.59, bf16[1,7,3584]{2,0,1:T(2,128)(2,1)} %collective-permute-done.12, s32[]{:T(128)S(6)} %select_n.27, s32[]{:T(128)} %constant.24.clone.1, s32[]{:T(128)} %constant.24.clone.1) | dynamic-update-slice | bytes 100356 | tf_op jit(solution)/shard_map/dynamic_update_slice | solution.py:23
  159.7 2.7 %dynamic_update_slice.61 = bf16[8,7,3584]{2,0,1:T(8,128)(2,1)S(1)} dynamic-update-slice(bf16[8,7,3584]{2,0,1:T(8,128)(2,1)S(1)} %dynamic_update_slice.60, bf16[1,7,3584]{2,0,1:T(2,128)(2,1)} %collective-permute-done.13, s32[]{:T(128)S(6)} %select_n.28, s32[]{:T(128)} %constant.24.clone.1, s32[]{:T(128)} %constant.24.clone.1) | dynamic-update-slice | bytes 100356 | tf_op jit(solution)/shard_map/dynamic_update_slice | solution.py:23
  162.3 2.7 %dynamic_update_slice.62 = bf16[8,7,3584]{2,0,1:T(8,128)(2,1)S(1)} dynamic-update-slice(bf16[8,7,3584]{2,0,1:T(8,128)(2,1)S(1)} %dynamic_update_slice.61, bf16[1,7,3584]{2,0,1:T(2,128)(2,1)} %collective-permute-done.14, s32[]{:T(128)S(6)} %select_n.29, s32[]{:T(128)} %constant.24.clone.1, s32[]{:T(128)} %constant.24.clone.1) | dynamic-update-slice | bytes 100356 | tf_op jit(solution)/shard_map/dynamic_update_slice | solution.py:23
  165.0 2.7 %dynamic_update_slice.63 = bf16[8,7,3584]{2,0,1:T(8,128)(2,1)S(1)} dynamic-update-slice(bf16[8,7,3584]{2,0,1:T(8,128)(2,1)S(1)} %dynamic_update_slice.62, bf16[1,7,3584]{2,0,1:T(2,128)(2,1)} %collective-permute-done.15, s32[]{:T(128)S(6)} %select_n.30, s32[]{:T(128)} %constant.24.clone.1, s32[]{:T(128)} %constant.24.clone.1) | dynamic-update-slice | bytes 100356 | tf_op jit(solution)/shard_map/dynamic_update_slice | solution.py:23
  169.1 2.2 %reduce_sum.138 = f32[4,7,3584]{2,0,1:T(4,128)S(1)} reduce(f32[4,2,7,3584]{3,1,0,2:T(2,128)} %reshape.192, f32[]{:T(128)} %constant.21.clone.1), dimensions={1}, to_apply=%region_16.18 | reduce | flops 100352 | bytes 1204228 | tf_op jit(solution)/shard_map/reduce_sum | solution.py:58
  180.6 4.2 %all-to-all-start.3 = ((bf16[8,7,3584]{2,1,0:T(8,128)(2,1)}), bf16[8,7,3584]{2,1,0:T(8,128)(2,1)S(1)}, u32[]{:S(2)}, u32[]{:S(2)}) async-start(bf16[8,7,3584]{2,1,0:T(8,128)(2,1)} %copy.32), calls=%async_computation.3 | async-start | bytes 917504 | tf_op jit(solution)/shard_map/all_to_all | solution.py:109
  187.3 6.6 %all-to-all-done.3 = bf16[8,7,3584]{2,1,0:T(8,128)(2,1)S(1)} async-done(((bf16[8,7,3584]{2,1,0:T(8,128)(2,1)}), bf16[8,7,3584]{2,1,0:T(8,128)(2,1)S(1)}, u32[]{:S(2)}, u32[]{:S(2)}) %all-to-all-start.3) | async-done | bytes 401440 | tf_op jit(solution)/shard_map/all_to_all | solution.py:109
  (219 shorter events, 85.9 us)
Async XLA Ops:
  0.6 26.5 %copy-start = (bf16[1,3584,128]{2,1,0:T(8,128)(2,1)S(1)}, bf16[1,3584,128]{2,1,0:T(8,128)(2,1)}, u32[]{:S(2)}) copy-start(bf16[1,3584,128]{2,1,0:T(8,128)(2,1)} %param.21) | copy-start | bytes 2752516
  5.7 9.7 %copy-start.8 = (f32[3584]{0:T(1024)}, f32[3584]{0:T(1024)S(1)}, u32[]{:S(2)}) copy-start(f32[3584]{0:T(1024)S(1)} %reduce) | copy-start | bytes 43012
  6.3 8.4 %copy-start.22 = (s32[24]{0:T(128)}, s32[24]{0:T(128)S(1)}, u32[]{:S(2)}) copy-start(s32[24]{0:T(128)S(1)} %get-tuple-element.6) | copy-start | bytes 292
  6.3 9.4 %copy-start.29 = (s32[24]{0:T(128)}, s32[24]{0:T(128)S(1)}, u32[]{:S(2)}) copy-start(s32[24]{0:T(128)S(1)} %get-tuple-element.48) | copy-start | bytes 292
  7.5 7.8 %copy-start.7 = (bf16[1,24,3584]{2,1,0:T(8,128)(2,1)S(1)}, bf16[1,24,3584]{2,1,0:T(8,128)(2,1)}, u32[]{:S(2)}) copy-start(bf16[1,24,3584]{2,1,0:T(8,128)(2,1)} %param.13) | copy-start | bytes 516100
  7.5 14.3 %all-to-all-start.5 = ((bf16[8,7,3584]{2,1,0:T(8,128)(2,1)}), bf16[8,7,3584]{2,1,0:T(8,128)(2,1)S(1)}, u32[]{:S(2)}, u32[]{:S(2)}) async-start(bf16[8,7,3584]{2,1,0:T(8,128)(2,1)} %bitcast.24), calls=%async_computation.5 | async-start | bytes 917504 | tf_op jit(solution)/shard_map/all_to_all | solution.py:110
  18.1 8.0 %copy-start.1 = (bf16[1,3584,128]{2,1,0:T(8,128)(2,1)S(1)}, bf16[1,3584,128]{2,1,0:T(8,128)(2,1)}, u32[]{:S(2)}) copy-start(bf16[1,3584,128]{2,1,0:T(8,128)(2,1)} %param.20) | copy-start | bytes 2752516
  22.6 12.4 %all-to-all-start.4 = ((bf16[8,7,3584]{2,1,0:T(8,128)(2,1)}), bf16[8,7,3584]{2,1,0:T(8,128)(2,1)S(1)}, u32[]{:S(2)}, u32[]{:S(2)}) async-start(bf16[8,7,3584]{2,1,0:T(8,128)(2,1)} %bitcast.22), calls=%async_computation.4 | async-start | bytes 917504 | tf_op jit(solution)/shard_map/all_to_all | solution.py:111
  28.0 12.4 %copy-start.2 = (bf16[1,128,3584]{2,1,0:T(8,128)(2,1)S(1)}, bf16[1,128,3584]{2,1,0:T(8,128)(2,1)}, u32[]{:S(2)}) copy-start(bf16[1,128,3584]{2,1,0:T(8,128)(2,1)} %param.22) | copy-start | bytes 2752516
  37.0 12.7 %all-to-all-start = ((bf16[8,7,3584]{2,1,0:T(8,128)(2,1)}), bf16[8,7,3584]{2,1,0:T(8,128)(2,1)S(1)}, u32[]{:S(2)}, u32[]{:S(2)}) async-start(bf16[8,7,3584]{2,1,0:T(8,128)(2,1)} %bitcast.129), calls=%async_computation | async-start | bytes 917504 | tf_op jit(solution)/shard_map/all_to_all | solution.py:96
  44.5 5.8 %collective-permute-start.1 = (bf16[1,7,3584]{2,0,1:T(2,128)(2,1)}, bf16[1,7,3584]{2,0,1:T(2,128)(2,1)}, u32[]{:S(2)}, u32[]{:S(2)}) collective-permute-start(bf16[1,7,3584]{2,0,1:T(2,128)(2,1)} %get-tuple-element.27), channel_id=1, source_target_pairs={{0,1},{1,0},{2,3},{3,2},{4,5},{5,4},{6,7},{7,6},{8,9},{9,8},{10,11... | collective-permute-start | bytes 150536 | tf_op jit(solution)/shard_map/ppermute | solution.py:22
  44.9 6.8 %collective-permute-start.2 = (bf16[1,7,3584]{2,0,1:T(2,128)(2,1)}, bf16[1,7,3584]{2,0,1:T(2,128)(2,1)}, u32[]{:S(2)}, u32[]{:S(2)}) collective-permute-start(bf16[1,7,3584]{2,0,1:T(2,128)(2,1)} %get-tuple-element.26), channel_id=1, source_target_pairs={{0,2},{1,3},{2,0},{3,1},{4,6},{5,7},{6,4},{7,5},{8,10},{9,11},{10,... | collective-permute-start | bytes 150536 | tf_op jit(solution)/shard_map/ppermute | solution.py:22
  46.5 18.9 %collective-permute-start.3 = (bf16[1,7,3584]{2,0,1:T(2,128)(2,1)}, bf16[1,7,3584]{2,0,1:T(2,128)(2,1)}, u32[]{:S(2)}, u32[]{:S(2)}) collective-permute-start(bf16[1,7,3584]{2,0,1:T(2,128)(2,1)} %get-tuple-element.25), channel_id=1, source_target_pairs={{0,3},{1,2},{2,1},{3,0},{4,7},{5,6},{6,5},{7,4},{8,11},{9,10},{10,... | collective-permute-start | bytes 150536 | tf_op jit(solution)/shard_map/ppermute | solution.py:22
  46.5 21.6 %collective-permute-start.4 = (bf16[1,7,3584]{2,0,1:T(2,128)(2,1)}, bf16[1,7,3584]{2,0,1:T(2,128)(2,1)}, u32[]{:S(2)}, u32[]{:S(2)}) collective-permute-start(bf16[1,7,3584]{2,0,1:T(2,128)(2,1)} %get-tuple-element.24), channel_id=1, source_target_pairs={{0,4},{1,5},{2,6},{3,7},{4,0},{5,1},{6,2},{7,3},{8,12},{9,13},{10,... | collective-permute-start | bytes 150536 | tf_op jit(solution)/shard_map/ppermute | solution.py:22
  48.3 22.5 %collective-permute-start.5 = (bf16[1,7,3584]{2,0,1:T(2,128)(2,1)}, bf16[1,7,3584]{2,0,1:T(2,128)(2,1)}, u32[]{:S(2)}, u32[]{:S(2)}) collective-permute-start(bf16[1,7,3584]{2,0,1:T(2,128)(2,1)} %get-tuple-element.23), channel_id=1, source_target_pairs={{0,5},{1,4},{2,7},{3,6},{4,1},{5,0},{6,3},{7,2},{8,13},{9,12},{10,... | collective-permute-start | bytes 150536 | tf_op jit(solution)/shard_map/ppermute | solution.py:22
  50.3 23.2 %collective-permute-start.6 = (bf16[1,7,3584]{2,0,1:T(2,128)(2,1)}, bf16[1,7,3584]{2,0,1:T(2,128)(2,1)}, u32[]{:S(2)}, u32[]{:S(2)}) collective-permute-start(bf16[1,7,3584]{2,0,1:T(2,128)(2,1)} %get-tuple-element.22), channel_id=1, source_target_pairs={{0,6},{1,7},{2,4},{3,5},{4,2},{5,3},{6,0},{7,1},{8,14},{9,15},{10,... | collective-permute-start | bytes 150536 | tf_op jit(solution)/shard_map/ppermute | solution.py:22
  51.7 24.5 %collective-permute-start.7 = (bf16[1,7,3584]{2,0,1:T(2,128)(2,1)}, bf16[1,7,3584]{2,0,1:T(2,128)(2,1)}, u32[]{:S(2)}, u32[]{:S(2)}) collective-permute-start(bf16[1,7,3584]{2,0,1:T(2,128)(2,1)} %get-tuple-element.21), channel_id=1, source_target_pairs={{0,7},{1,6},{2,5},{3,4},{4,3},{5,2},{6,1},{7,0},{8,15},{9,14},{10,... | collective-permute-start | bytes 150536 | tf_op jit(solution)/shard_map/ppermute | solution.py:22
  53.3 47.1 %all-to-all-start.1 = ((bf16[8,7,3584]{2,1,0:T(8,128)(2,1)}), bf16[8,7,3584]{2,1,0:T(8,128)(2,1)}, u32[]{:S(2)}, u32[]{:S(2)}) async-start(bf16[8,7,3584]{2,1,0:T(8,128)(2,1)} %copy.27), calls=%async_computation.1 | async-start | bytes 917504 | tf_op jit(solution)/shard_map/all_to_all | solution.py:109
  89.5 8.9 %collective-permute-start.8 = (bf16[24,3584]{1,0:T(8,128)(2,1)}, bf16[24,3584]{1,0:T(8,128)(2,1)}, u32[]{:S(2)}, u32[]{:S(2)}) collective-permute-start(bf16[24,3584]{1,0:T(8,128)(2,1)} %fusion.33), channel_id=1, source_target_pairs={{8,0},{16,8},{24,16},{9,1},{17,9},{25,17},{10,2},{18,10},{26,18},{... | collective-permute-start | bytes 516104 | tf_op jit(solution)/shard_map/ppermute | solution.py:30
  101.1 15.5 %all-to-all-start.7 = ((bf16[8,7,3584]{2,1,0:T(8,128)(2,1)}), bf16[8,7,3584]{2,1,0:T(8,128)(2,1)}, u32[]{:S(2)}, u32[]{:S(2)}) async-start(bf16[8,7,3584]{2,1,0:T(8,128)(2,1)} %bitcast.30), calls=%async_computation.7 | async-start | bytes 917504 | tf_op jit(solution)/shard_map/all_to_all | solution.py:110
  112.5 12.8 %collective-permute-start = (bf16[24,3584]{1,0:T(8,128)(2,1)}, bf16[24,3584]{1,0:T(8,128)(2,1)}, u32[]{:S(2)}, u32[]{:S(2)}) collective-permute-start(bf16[24,3584]{1,0:T(8,128)(2,1)} %fusion.41), channel_id=1, source_target_pairs={{0,8},{8,16},{16,24},{1,9},{9,17},{17,25},{2,10},{10,18},{18,26},{... | collective-permute-start | bytes 516104 | tf_op jit(solution)/shard_map/ppermute | solution.py:30
  117.4 12.9 %all-to-all-start.6 = ((bf16[8,7,3584]{2,1,0:T(8,128)(2,1)}), bf16[8,7,3584]{2,1,0:T(8,128)(2,1)S(1)}, u32[]{:S(2)}, u32[]{:S(2)}) async-start(bf16[8,7,3584]{2,1,0:T(8,128)(2,1)} %bitcast.130), calls=%async_computation.6 | async-start | bytes 917504 | tf_op jit(solution)/shard_map/all_to_all | solution.py:111
  132.0 8.0 %copy-start.10 = (f32[3584]{0:T(1024)S(1)}, f32[3584]{0:T(1024)}, u32[]{:S(2)}) copy-start(f32[3584]{0:T(1024)} %copy-done.8) | copy-start | bytes 43012
  133.6 3.6 %collective-permute-start.9 = (bf16[1,7,3584]{2,0,1:T(2,128)(2,1)S(1)}, bf16[1,7,3584]{2,0,1:T(2,128)(2,1)S(1)}, u32[]{:S(2)}, u32[]{:S(2)}) collective-permute-start(bf16[1,7,3584]{2,0,1:T(2,128)(2,1)S(1)} %get-tuple-element.19), channel_id=1, source_target_pairs={{0,1},{1,0},{2,3},{3,2},{4,5},{5,4},{6,7},{7,6},{8,9},{9,8},{10,11... | collective-permute-start | bytes 150536 | tf_op jit(solution)/shard_map/ppermute | solution.py:22
  133.6 5.8 %collective-permute-start.10 = (bf16[1,7,3584]{2,0,1:T(2,128)(2,1)S(1)}, bf16[1,7,3584]{2,0,1:T(2,128)(2,1)S(1)}, u32[]{:S(2)}, u32[]{:S(2)}) collective-permute-start(bf16[1,7,3584]{2,0,1:T(2,128)(2,1)S(1)} %get-tuple-element.18), channel_id=1, source_target_pairs={{0,2},{1,3},{2,0},{3,1},{4,6},{5,7},{6,4},{7,5},{8,10},{9,11},{10,... | collective-permute-start | bytes 150536 | tf_op jit(solution)/shard_map/ppermute | solution.py:22
  134.3 20.0 %collective-permute-start.11 = (bf16[1,7,3584]{2,0,1:T(2,128)(2,1)}, bf16[1,7,3584]{2,0,1:T(2,128)(2,1)}, u32[]{:S(2)}, u32[]{:S(2)}) collective-permute-start(bf16[1,7,3584]{2,0,1:T(2,128)(2,1)} %get-tuple-element.17), channel_id=1, source_target_pairs={{0,3},{1,2},{2,1},{3,0},{4,7},{5,6},{6,5},{7,4},{8,11},{9,10},{10,... | collective-permute-start | bytes 150536 | tf_op jit(solution)/shard_map/ppermute | solution.py:22
  135.5 21.5 %collective-permute-start.12 = (bf16[1,7,3584]{2,0,1:T(2,128)(2,1)}, bf16[1,7,3584]{2,0,1:T(2,128)(2,1)}, u32[]{:S(2)}, u32[]{:S(2)}) collective-permute-start(bf16[1,7,3584]{2,0,1:T(2,128)(2,1)} %get-tuple-element.16), channel_id=1, source_target_pairs={{0,4},{1,5},{2,6},{3,7},{4,0},{5,1},{6,2},{7,3},{8,12},{9,13},{10,... | collective-permute-start | bytes 150536 | tf_op jit(solution)/shard_map/ppermute | solution.py:22
  136.0 23.6 %collective-permute-start.13 = (bf16[1,7,3584]{2,0,1:T(2,128)(2,1)}, bf16[1,7,3584]{2,0,1:T(2,128)(2,1)}, u32[]{:S(2)}, u32[]{:S(2)}) collective-permute-start(bf16[1,7,3584]{2,0,1:T(2,128)(2,1)} %get-tuple-element.15), channel_id=1, source_target_pairs={{0,5},{1,4},{2,7},{3,6},{4,1},{5,0},{6,3},{7,2},{8,13},{9,12},{10,... | collective-permute-start | bytes 150536 | tf_op jit(solution)/shard_map/ppermute | solution.py:22
  137.2 25.2 %collective-permute-start.14 = (bf16[1,7,3584]{2,0,1:T(2,128)(2,1)}, bf16[1,7,3584]{2,0,1:T(2,128)(2,1)}, u32[]{:S(2)}, u32[]{:S(2)}) collective-permute-start(bf16[1,7,3584]{2,0,1:T(2,128)(2,1)} %get-tuple-element.14), channel_id=1, source_target_pairs={{0,6},{1,7},{2,4},{3,5},{4,2},{5,3},{6,0},{7,1},{8,14},{9,15},{10,... | collective-permute-start | bytes 150536 | tf_op jit(solution)/shard_map/ppermute | solution.py:22
  139.4 25.7 %collective-permute-start.15 = (bf16[1,7,3584]{2,0,1:T(2,128)(2,1)}, bf16[1,7,3584]{2,0,1:T(2,128)(2,1)}, u32[]{:S(2)}, u32[]{:S(2)}) collective-permute-start(bf16[1,7,3584]{2,0,1:T(2,128)(2,1)} %get-tuple-element.13), channel_id=1, source_target_pairs={{0,7},{1,6},{2,5},{3,4},{4,3},{5,2},{6,1},{7,0},{8,15},{9,14},{10,... | collective-permute-start | bytes 150536 | tf_op jit(solution)/shard_map/ppermute | solution.py:22
  142.1 34.7 %all-to-all-start.2 = ((bf16[8,7,3584]{2,1,0:T(8,128)(2,1)}), bf16[8,7,3584]{2,1,0:T(8,128)(2,1)}, u32[]{:S(2)}, u32[]{:S(2)}) async-start(bf16[8,7,3584]{2,1,0:T(8,128)(2,1)} %bitcast.14), calls=%async_computation.2 | async-start | bytes 917504 | tf_op jit(solution)/shard_map/all_to_all | solution.py:96
  180.6 13.2 %all-to-all-start.3 = ((bf16[8,7,3584]{2,1,0:T(8,128)(2,1)}), bf16[8,7,3584]{2,1,0:T(8,128)(2,1)S(1)}, u32[]{:S(2)}, u32[]{:S(2)}) async-start(bf16[8,7,3584]{2,1,0:T(8,128)(2,1)} %copy.32), calls=%async_computation.3 | async-start | bytes 917504 | tf_op jit(solution)/shard_map/all_to_all | solution.py:109
  (37 other events, 64.7 us)
